TPU v7x, 32 devices: a whole 2x2x4 slice. The times are simulated.
32 devices in a mesh: dom: 8 (over z, y), rep: 4 (over x, core).
Axes of the slice: x: 2, y: 2, z: 4, core: 2. Of those that a mesh axis runs over, the one named last changes fastest.
Arguments:
- feats: bfloat16 [256, 32768], P('rep', 'dom'), may hold values from -6 to 6
- w_self: bfloat16 [256, 256], P(None, 'rep'), may hold values from -0.375 to 0.375
- w_neigh: bfloat16 [256, 256], P(None, 'rep'), may hold values from -3 to 3
- local_cols: int32 [256, 2], P('dom'), may hold values from 0 to 31
- local_tiles: bfloat16 [256, 2, 128, 128], P('dom'), may hold values from 0 to 3, as said below
- send_list: int32 [8, 8, 2], P('dom'), may hold values from 0 to 31
- remote_rows: int32 [8, 8, 2], P('dom'), may hold values from 0 to 31
- remote_tiles: bfloat16 [8, 8, 2, 128, 128], P('dom'), may hold values from 0 to 3, as said below
- cotangent: bfloat16 [256, 32768], P('rep', 'dom'), may hold values from -6 to 6
Outputs:
- output: bfloat16 [256, 32768], P('rep', 'dom')
- grad_feats: bfloat16 [256, 32768], P('rep', 'dom')
- grad_w_self: float32 [256, 256], P(None, 'rep')
- grad_w_neigh: float32 [256, 256], P(None, 'rep')
Inputs may be any that keep to these rules, and one draw needn't show every extreme that they name: `local_tiles`: edge weights: zero where a tile has no edge, positive otherwise. `remote_tiles`: edge weights: zero where a tile has no edge, positive otherwise.
All inputs are finite; a program needn't handle non-finite values.
Results may differ from a plain program's by a relative error of at most 0.0055.
Values may be sent and summed in bfloat16 or wider, within the bound.
A program may use at most 128 MiB of HBM per device.

v0:
```python
import jax
import jax.numpy as jnp
from jax import lax
from jax.sharding import PartitionSpec as P


def local(
    feats, w_self, w_neigh, local_cols, local_tiles, send_list, remote_rows, remote_tiles, cotangent
):
    highest = lax.Precision.HIGHEST
    feat_width, node_count = feats.shape
    blocks, local_links, tile_side, _ = local_tiles.shape
    block_ids = jnp.arange(blocks, dtype=jnp.int32)
    blocked = feats.reshape(feat_width, blocks, tile_side)
    outgoing = blocked[:, send_list[0]]
    incoming = lax.all_to_all(outgoing, "dom", split_axis=1, concat_axis=1, tiled=True)
    full_feats = lax.all_gather(feats, "rep", axis=0, tiled=True)
    gathered = blocked[:, local_cols]
    summed = jnp.einsum("fblj,blij->fbi", gathered, local_tiles, preferred_element_type=jnp.float32)
    weight_rows = jnp.sum(local_tiles, axis=(1, 3), dtype=jnp.float32)
    far_tiles = remote_tiles[0]
    far_rows = remote_rows[0]
    placing = (far_rows[:, :, None] == block_ids).astype(jnp.float32)
    far_sums = jnp.sum(far_tiles, axis=3, dtype=jnp.float32)
    divisor = 1.0 + weight_rows + jnp.einsum("ski,skb->bi", far_sums, placing, precision=highest)
    far_terms = jnp.einsum(
        "fskj,skij->fski", incoming, far_tiles, preferred_element_type=jnp.float32
    )
    summed = summed + jnp.einsum("fski,skb->fbi", far_terms, placing, precision=highest)
    aggregate = (summed / divisor).astype(jnp.bfloat16).reshape(feat_width, node_count)
    full_agg = lax.all_gather(aggregate, "rep", axis=0, tiled=True)
    preact = jnp.einsum("ab,an->bn", w_self, full_feats, preferred_element_type=jnp.float32)
    preact = preact + jnp.einsum("ab,an->bn", w_neigh, full_agg, preferred_element_type=jnp.float32)
    sigmoid_val = jax.nn.sigmoid(preact)
    output = (preact * sigmoid_val).astype(jnp.bfloat16)
    slope = sigmoid_val * (1.0 + preact * (1.0 - sigmoid_val))
    grad_pre = (cotangent.astype(jnp.float32) * slope).astype(jnp.bfloat16)
    wg_self = jnp.einsum("an,bn->ab", full_feats, grad_pre, preferred_element_type=jnp.float32)
    wg_neigh = jnp.einsum("an,bn->ab", full_agg, grad_pre, preferred_element_type=jnp.float32)
    wg_self, wg_neigh = lax.psum((wg_self, wg_neigh), "dom")
    whole_self, whole_neigh = (
        lax.all_gather(w_self, "rep", axis=1, tiled=True),
        lax.all_gather(w_neigh, "rep", axis=1, tiled=True),
    )
    offset = lax.axis_index("rep") * feat_width
    mine_self = lax.dynamic_slice_in_dim(whole_self, offset, feat_width, 0)
    mine_neigh = lax.dynamic_slice_in_dim(whole_neigh, offset, feat_width, 0)
    shard_rows = lax.all_gather(grad_pre, "rep", axis=0, tiled=True)
    back_self = jnp.dot(mine_self, shard_rows, preferred_element_type=jnp.float32)
    back_agg = jnp.dot(mine_neigh, shard_rows, preferred_element_type=jnp.float32)
    scaled = (back_agg.reshape(feat_width, blocks, tile_side) / divisor).astype(jnp.bfloat16)
    picked = scaled[:, far_rows]
    far_back = jnp.einsum("fski,skij->fskj", picked, far_tiles, preferred_element_type=jnp.float32)
    returned = lax.all_to_all(far_back, "dom", split_axis=1, concat_axis=1, tiled=True)
    near_back = jnp.einsum(
        "fbi,blij->fblj", scaled, local_tiles, preferred_element_type=jnp.float32
    )
    landing = (local_cols[:, :, None] == block_ids).astype(jnp.float32)
    collected = jnp.einsum("fblj,blc->fcj", near_back, landing, precision=highest)
    homing = (send_list[0][:, :, None] == block_ids).astype(jnp.float32)
    collected = collected + jnp.einsum("fdkj,dkc->fcj", returned, homing, precision=highest)
    grad_feats = (back_self + collected.reshape(feat_width, node_count)).astype(jnp.bfloat16)
    return (output, grad_feats, wg_self, wg_neigh)


def solution(mesh):
    placed = (
        P("rep", "dom"),
        P(None, "rep"),
        P(None, "rep"),
        P("dom", None),
        P("dom", None, None, None),
        P("dom", None, None),
        P("dom", None, None),
        P("dom", None, None, None, None),
        P("rep", "dom"),
    )
    return jax.shard_map(
        local,
        mesh=mesh,
        in_specs=placed,
        out_specs=(P("rep", "dom"), P("rep", "dom"), P(None, "rep"), P(None, "rep")),
        check_vma=False,
    )
```

profile of v0, /device:TPU:0, one launch (start us, length us, event | category | flops | bytes accessed | tf_op | source)
XLA Modules:
  0.0 199.6 jit_solution(13848253110576622706)
XLA Ops:
  7.2 0.0 copy-start.9
  7.2 0.0 copy-start.2
  7.2 0.7 compare_select_fusion.1
  7.9 0.1 copy.37
  8.0 0.1 reshape.94
  8.1 1.2 copy_bitcast_fusion.1
  9.3 0.0 copy-start
  9.3 1.3 gather_fusion.1
  10.6 7.3 %all-to-all-start = ((bf16[64,8,2,128]{3,0,2,1:T(8,128)(2,1)}), bf16[64,8,2,128]{3,0,2,1:T(8,128)(2,1)S(1)}, u32[]{:S(2)}, u32[]{:S(2)}) async-start(bf16[64,8,2,128]{3,0,2,1:T(8,128)(2,1)} %bitcast.115), calls=%async_computation | async-start | bytes 524288 | tf_op jit(solution)/shard_map/all_to_all | solution.py:16
  17.9 0.0 all-gather.6.cloned.1.call-start
  17.9 0.0 copy-done.9
  18.0 0.0 copy-done.2
  18.0 0.2 convert_reduce_fusion.1
  18.2 0.1 copy.35
  18.3 0.1 reshape.86
  18.4 0.0 copy-start.12
  18.4 1.7 gather_fusion
  20.1 0.6 convert_reduce_fusion
  20.7 0.0 copy-done.12
  20.7 0.3 fusion.11
  21.0 5.8 %all-to-all-done = bf16[64,8,2,128]{3,0,2,1:T(8,128)(2,1)S(1)} async-done(((bf16[64,8,2,128]{3,0,2,1:T(8,128)(2,1)}), bf16[64,8,2,128]{3,0,2,1:T(8,128)(2,1)S(1)}, u32[]{:S(2)}, u32[]{:S(2)}) %all-to-all-start) | async-done | bytes 262176 | tf_op jit(solution)/shard_map/all_to_all | solution.py:16
  26.8 0.4 convolution_bitcast_fusion.7
  27.3 0.9 convolution_bitcast_fusion.5
  28.2 0.0 copy-done.6
  28.2 1.1 fusion.10
  29.3 0.0 copy-start.7
  29.3 0.9 copy.71
  30.2 0.0 all-gather.6.cloned.1.call-update
  30.2 0.0 all-gather.4.cloned.1.call-start
  30.3 0.7 all-gather.4.cloned.1.call-update
  31.0 0.0 all-gather.8.cloned.1.call-start
  31.0 20.9 %all-gather.6.cloned.1.call-done = bf16[256,4096]{1,0:T(8,128)(2,1)} async-done(((bf16[64,4096]{1,0:T(8,128)(2,1)}), bf16[256,4096]{1,0:T(8,128)(2,1)}) %all-gather.6.cloned.1.call-update) | async-done | bytes 2097168 | tf_op jit(solution)/shard_map/all_gather | solution.py:31
  51.9 0.0 copy-done.7
  51.9 3.1 %convolution_bitcast_fusion = f32[64,4096]{1,0:T(8,128)} fusion(bf16[256,64]{0,1:T(8,128)(2,1)S(1)} %copy-done.7, bf16[256,4096]{1,0:T(8,128)(2,1)} %all-gather.6.cloned.1.call-done), kind=kOutput, calls=%fused_computation.5 | convolution fusion | flops 134217728 | bytes 3178496 | tf_op jit(solution)/shard_map/ab,an->bn/dot_general | solution.py:33
  55.0 21.1 %all-gather.4.cloned.1.call-done = bf16[256,4096]{1,0:T(8,128)(2,1)} async-done(((bf16[64,4096]{1,0:T(8,128)(2,1)}), bf16[256,4096]{1,0:T(8,128)(2,1)}) %all-gather.4.cloned.1.call-update) | async-done | bytes 2097168 | tf_op jit(solution)/shard_map/all_gather | solution.py:17
  76.1 0.0 copy-done.8
  76.1 3.6 %multiply_convert_fusion = (bf16[64,4096]{1,0:T(8,128)(2,1)}, bf16[64,4096]{1,0:T(8,128)(2,1)}) fusion(bf16[64,4096]{1,0:T(8,128)(2,1)S(1)} %copy-done.13, f32[64,4096]{1,0:T(8,128)} %convolution_bitcast_fusion, bf16[256,64]{0,1:T(8,128)(2,1)S(1)} %copy-done.8, bf16[256,4096]{1,0:T(8,128)(2,1)} %all-gather.4.cloned.1.call-done), kind=kOutput, calls=%fused_computation.28 | convolution fusion | flops 137625600 | bytes 4751360 | tf_op jit(solution)/shard_map/ab,an->bn/dot_general | solution.py:32
  79.7 0.0 all-gather.8.cloned.1.call-update
  79.7 0.1 copy.45
  79.8 0.1 reshape.102
  79.9 5.4 %all_gather.17 = bf16[256,256]{0,1:T(8,128)(2,1)S(1)} all-gather(bf16[256,64]{0,1:T(8,128)(2,1)S(1)} %copy-done.8), channel_id=1, replica_groups=mesh['dom'=8,'rep'=4] {'rep'}, dimensions={1}, use_global_device_ids=true | all-gather | bytes 163840 | tf_op jit(solution)/shard_map/all_gather | solution.py:42
  85.3 5.6 %all_gather.19 = bf16[256,256]{0,1:T(8,128)(2,1)S(1)} all-gather(bf16[256,64]{0,1:T(8,128)(2,1)S(1)} %copy-done.7), channel_id=1, replica_groups=mesh['dom'=8,'rep'=4] {'rep'}, dimensions={1}, use_global_device_ids=true | all-gather | bytes 163840 | tf_op jit(solution)/shard_map/all_gather | solution.py:43
  90.9 0.6 pad_clamp_fusion
  91.5 11.1 %all-gather.8.cloned.1.call-done = bf16[256,4096]{1,0:T(8,128)(2,1)} async-done(((bf16[64,4096]{1,0:T(8,128)(2,1)}), bf16[256,4096]{1,0:T(8,128)(2,1)}) %all-gather.8.cloned.1.call-update) | async-done | bytes 2097168 | tf_op jit(solution)/shard_map/all_gather | solution.py:48
  102.6 2.2 %convolution_bitcast_fusion.2 = f32[8,32,8,128]{3,2,1,0:T(8,128)S(1)} fusion(bf16[256,4096]{1,0:T(8,128)(2,1)} %all-gather.8.cloned.1.call-done, bf16[256,256]{0,1:T(8,128)(2,1)S(1)} %all_gather.19, s32[]{:T(128)S(6)} %select_n.29), kind=kOutput, calls=%fused_computation.12 | convolution fusion | flops 134217728 | bytes 3211268 | tf_op jit(solution)/shard_map/dot_general | solution.py:50
  104.8 0.0 copy-start.3
  104.8 0.9 fusion.12
  105.8 1.8 gather_fusion.2
  107.5 1.1 convolution_bitcast_fusion.6
  108.6 5.5 %all-to-all-start.1 = ((f32[64,8,2,128]{3,0,2,1:T(8,128)}), f32[64,8,2,128]{3,0,2,1:T(8,128)}, u32[]{:S(2)}, u32[]{:S(2)}) async-start(f32[64,8,2,128]{3,0,2,1:T(8,128)} %convolution_bitcast_fusion.6), calls=%async_computation.1 | async-start | bytes 1048576 | tf_op jit(solution)/shard_map/all_to_all | solution.py:54
  114.1 0.0 all-reduce.3.cloned.1.call-start
  114.2 3.1 %fusion.33 = f32[256,64]{0,1:T(8,128)} fusion(bf16[256,4096]{1,0:T(8,128)(2,1)} %all-gather.6.cloned.1.call-done, bf16[64,4096]{1,0:T(8,128)(2,1)S(1)} %copy-done.3), kind=kOutput, calls=%fused_computation.60 | convolution fusion | flops 134217728 | bytes 2686976 | tf_op jit(solution)/shard_map/an,bn->ab/dot_general | solution.py:39
  117.3 1.4 convolution_bitcast_fusion.8
  118.7 0.0 all-reduce.3.cloned.1.call-update
  118.7 0.0 copy-start.10
  118.8 0.4 convolution_bitcast_fusion.1
  119.2 0.2 copy-done.10
  119.4 2.1 %fusion.3 = f32[32,64,128]{2,0,1:T(8,128)S(1)} fusion(f32[64,32,2,128]{3,0,2,1:T(8,128)S(1)} %convolution_bitcast_fusion.1, s32[32,2]{0,1:T(2,128)S(1)} %copy-done.10), kind=kOutput, calls=%fused_computation.11 | convolution fusion | flops 201328640 | bytes 3145984 | tf_op jit(solution)/shard_map/fblj,blc->fcj/dot_general | solution.py:59
  121.5 8.1 %all-to-all-done.1 = f32[64,8,2,128]{3,0,2,1:T(8,128)} async-done(((f32[64,8,2,128]{3,0,2,1:T(8,128)}), f32[64,8,2,128]{3,0,2,1:T(8,128)}, u32[]{:S(2)}, u32[]{:S(2)}) %all-to-all-start.1) | async-done | bytes 524320 | tf_op jit(solution)/shard_map/all_to_all | solution.py:54
  129.6 1.9 fusion.8
  131.5 1.8 fusion
  133.3 56.8 %all-reduce.3.cloned.1.call-done = (f32[256,64]{0,1:T(8,128)}, f32[256,64]{0,1:T(8,128)}) async-done(((f32[256,64]{0,1:T(8,128)}, f32[256,64]{0,1:T(8,128)}), (f32[256,64]{0,1:T(8,128)}, f32[256,64]{0,1:T(8,128)})) %all-reduce.3.cloned.1.call-update) | async-done | bytes 131088 | tf_op jit(solution)/shard_map/psum | solution.py:40
  190.1 1.5 copy.74
  191.6 1.5 copy.75
  (18 shorter events, 0.0 us)
Async XLA Ops:
  7.2 10.8 %copy-start.9 = (s32[32,2]{0,1:T(2,128)S(1)}, s32[32,2]{0,1:T(2,128)}, u32[]{:S(2)}) copy-start(s32[32,2]{0,1:T(2,128)} %param.12) | copy-start | bytes 772
  7.2 10.8 %copy-start.2 = (bf16[1,8,2,128,128]{4,3,2,1,0:T(8,128)(2,1)S(1)}, bf16[1,8,2,128,128]{4,3,2,1,0:T(8,128)(2,1)}, u32[]{:S(2)}) copy-start(bf16[1,8,2,128,128]{4,3,2,1,0:T(8,128)(2,1)} %param.16) | copy-start | bytes 1572868
  9.3 10.8 %copy-start = (bf16[32,2,128,128]{3,2,1,0:T(8,128)(2,1)S(1)}, bf16[32,2,128,128]{3,2,1,0:T(8,128)(2,1)}, u32[]{:S(2)}) copy-start(bf16[32,2,128,128]{3,2,1,0:T(8,128)(2,1)} %param.13) | copy-start | bytes 6291460
  10.6 16.2 %all-to-all-start = ((bf16[64,8,2,128]{3,0,2,1:T(8,128)(2,1)}), bf16[64,8,2,128]{3,0,2,1:T(8,128)(2,1)S(1)}, u32[]{:S(2)}, u32[]{:S(2)}) async-start(bf16[64,8,2,128]{3,0,2,1:T(8,128)(2,1)} %bitcast.115), calls=%async_computation | async-start | bytes 524288 | tf_op jit(solution)/shard_map/all_to_all | solution.py:16
  17.9 34.1 %all-gather.6.cloned.1.call-start = ((), (), s32[]{:S(2)}) async-start(), calls=%async_computation.3 | async-start | bytes 2621440 | tf_op jit(solution)/shard_map/all_gather | solution.py:31
  18.4 2.3 %copy-start.12 = (s32[1,8,2]{1,2,0:T(2,128)S(1)}, s32[1,8,2]{1,2,0:T(2,128)}, u32[]{:S(2)}) copy-start(s32[1,8,2]{1,2,0:T(2,128)} %param.15) | copy-start | bytes 196
  26.8 1.4 copy-start.6
  29.3 22.6 %copy-start.7 = (bf16[256,64]{0,1:T(8,128)(2,1)S(1)}, bf16[256,64]{0,1:T(8,128)(2,1)}, u32[]{:S(2)}) copy-start(bf16[256,64]{0,1:T(8,128)(2,1)} %param.11) | copy-start | bytes 98308
  30.2 45.9 %copy-start.8 = (bf16[256,64]{0,1:T(8,128)(2,1)S(1)}, bf16[256,64]{0,1:T(8,128)(2,1)}, u32[]{:S(2)}) copy-start(bf16[256,64]{0,1:T(8,128)(2,1)} %param.10) | copy-start | bytes 98308
  30.2 45.9 %copy-start.13 = (bf16[64,4096]{1,0:T(8,128)(2,1)S(1)}, bf16[64,4096]{1,0:T(8,128)(2,1)}, u32[]{:S(2)}) copy-start(bf16[64,4096]{1,0:T(8,128)(2,1)} %param.17) | copy-start | bytes 1572868
  30.2 45.9 %all-gather.4.cloned.1.call-start = ((), (), s32[]{:S(2)}) async-start(), calls=%async_computation.2 | async-start | bytes 2621440 | tf_op jit(solution)/shard_map/all_gather | solution.py:17
  31.0 71.7 %all-gather.8.cloned.1.call-start = ((), (), s32[]{:S(2)}) async-start(), calls=%async_computation.4 | async-start | bytes 2621440 | tf_op jit(solution)/shard_map/all_gather | solution.py:48
  104.8 9.3 %copy-start.3 = (bf16[64,4096]{1,0:T(8,128)(2,1)S(1)}, bf16[64,4096]{1,0:T(8,128)(2,1)}, u32[]{:S(2)}) copy-start(bf16[64,4096]{1,0:T(8,128)(2,1)} %get-tuple-element.6) | copy-start | bytes 1572868
  108.6 21.0 %all-to-all-start.1 = ((f32[64,8,2,128]{3,0,2,1:T(8,128)}), f32[64,8,2,128]{3,0,2,1:T(8,128)}, u32[]{:S(2)}, u32[]{:S(2)}) async-start(f32[64,8,2,128]{3,0,2,1:T(8,128)} %convolution_bitcast_fusion.6), calls=%async_computation.1 | async-start | bytes 1048576 | tf_op jit(solution)/shard_map/all_to_all | solution.py:54
  114.1 4.6 %copy-start.4 = (bf16[64,32,128]{2,0,1:T(8,128)(2,1)S(1)}, bf16[64,32,128]{2,0,1:T(8,128)(2,1)}, u32[]{:S(2)}) copy-start(bf16[64,32,128]{2,0,1:T(8,128)(2,1)} %fusion.12) | copy-start | bytes 1572868
  114.1 76.0 %all-reduce.3.cloned.1.call-start = ((), (), s32[]{:S(2)}) async-start(), calls=%async_computation.5 | async-start | bytes 262144 | tf_op jit(solution)/shard_map/psum | solution.py:40
  114.2 3.1 %copy-start.5 = (bf16[256,4096]{1,0:T(8,128)(2,1)S(1)}, bf16[256,4096]{1,0:T(8,128)(2,1)}, u32[]{:S(2)}) copy-start(bf16[256,4096]{1,0:T(8,128)(2,1)} %all-gather.4.cloned.1.call-done) | copy-start | bytes 6291460
  118.7 0.7 copy-start.10
  119.4 10.2 %copy-start.11 = (s32[1,8,2]{1,2,0:T(2,128)S(1)}, s32[1,8,2]{1,2,0:T(2,128)}, u32[]{:S(2)}) copy-start(s32[1,8,2]{1,2,0:T(2,128)} %param.14) | copy-start | bytes 196
  121.5 10.0 %copy-start.1 = (bf16[256,4096]{1,0:T(8,128)(2,1)S(1)}, bf16[256,4096]{1,0:T(8,128)(2,1)}, u32[]{:S(2)}) copy-start(bf16[256,4096]{1,0:T(8,128)(2,1)} %all-gather.8.cloned.1.call-done) | copy-start | bytes 6291460
Sparse Core Ops, SparseCore 0:
  30.3 21.5 all-gather.5
  53.5 22.5 all-gather.3
  79.8 22.7 all-gather.7
  118.9 71.2 all-reduce.2
where the time goes:
time: 200 us
  waiting for transfers between devices  125 us (62%)
  matrix products  23.3 us (12%)
  between operations  14 us (7%)
  starting transfers between devices  13 us (6%)
  blocking collectives  11 us (6%)
  local copies, waits for them, and re-layouts  10.5 us (5%)
  other arithmetic  3.12 us (2%)
    psum x1, waiting for transfers between devices, local(): wg_self, wg_neigh = lax.psum((wg_self, wg_neigh), 'dom')  56.8 us
    all_gather x1, waiting for transfers between devices, local(): full_feats = lax.all_gather(feats, 'rep', axis=0, tiled=True)  21.1 us
    all_gather x1, waiting for transfers between devices, local(): full_agg = lax.all_gather(aggregate, 'rep', axis=0, tiled=True)  20.9 us
    all_gather x1, waiting for transfers between devices, local(): shard_rows = lax.all_gather(grad_pre, 'rep', axis=0, tiled=True)  11.1 us
    all_to_all x1, waiting for transfers between devices, local(): lax.all_to_all(far_back, 'dom', split_axis=1, concat_axis=1, tiled=True)  8.12 us
    all_to_all x1, starting transfers between devices, local(): lax.all_to_all(outgoing, 'dom', split_axis=1, concat_axis=1, tiled=True)  7.31 us
    all_to_all x1, waiting for transfers between devices, local(): lax.all_to_all(outgoing, 'dom', split_axis=1, concat_axis=1, tiled=True)  5.82 us
    all_gather x1, blocking collectives, local(): lax.all_gather(w_neigh, 'rep', axis=1, tiled=True)  5.6 us
  transfers between devices with their start and end apart: 6, of which 6 were waited for; matrix products, arithmetic and copies ran while one was open for 9% of the time, Pallas kernels for 0%

commit v1 on v0

v1 whole, which is shorter than its diff:
```python
import functools

import jax
import jax.numpy as jnp
from jax import lax
from jax.experimental import pallas as pl
from jax.experimental.pallas import tpu as pltpu
from jax.sharding import PartitionSpec as P

MESH = pl.DeviceIdType.MESH
F32 = jnp.float32
BF16 = jnp.bfloat16
CHUNKS = 4
ONES = 16
KEEP = 8
NT = (((1,), (1,)), ((), ()))


def mm(a, b):
    return jnp.dot(a, b, preferred_element_type=F32)


def mm_nt(a, b):
    return lax.dot_general(a, b, NT, preferred_element_type=F32)


def rcopy(src, dst, send, recv, dom, rep):
    return pltpu.make_async_remote_copy(
        src_ref=src,
        dst_ref=dst,
        send_sem=send,
        recv_sem=recv,
        device_id={"dom": dom, "rep": rep},
        device_id_type=MESH,
    )


def greet(devices):
    barrier = pltpu.get_barrier_semaphore()
    for dom, rep in devices:
        pl.semaphore_signal(
            barrier, inc=1, device_id={"dom": dom, "rep": rep}, device_id_type=MESH
        )
    pl.semaphore_wait(barrier, len(devices))


def main_kernel(
    D,
    R,
    feats,
    wts_in,
    wtn_in,
    cols,
    slist,
    place_at,
    ltiles_h,
    rtiles_h,
    cot_h,
    out_o,
    scaled_o,
    bself_o,
    gw_o,
    ltiles,
    rtiles,
    cot,
    blocks_of,
    hsend,
    hrecv,
    summed,
    far,
    inv,
    wts,
    wtn,
    wb,
    xf,
    xa,
    own,
    psend,
    precv,
    gp,
    loc_sem,
    h_s,
    h_r,
    ws_s,
    ws_r,
    wn_s,
    wn_r,
    xf_s,
    xf_r,
    xa_s,
    xa_r,
    pp_s,
    pp_r,
    gx_s,
    gx_r,
    gc_s,
    gc_r,
):
    d, r = lax.axis_index("dom"), lax.axis_index("rep")
    G = R // 2
    c, g = lax.rem(r, 2), lax.div(r, 2)
    mate = g * 2 + 1 - c
    F, N = feats.shape
    B, L, T, _ = ltiles.shape
    K = slist.shape[1]
    CH = N // CHUNKS
    CB = B // CHUNKS

    def cross(q):
        return lax.rem(g + q, G) * 2 + c

    loads = [
        pltpu.make_async_copy(ltiles_h, ltiles, loc_sem.at[0]),
        pltpu.make_async_copy(rtiles_h, rtiles, loc_sem.at[1]),
        pltpu.make_async_copy(cot_h, cot, loc_sem.at[2]),
    ]
    for load in loads:
        load.start()
    for b in range(B):
        blocks_of[b] = feats[:, b * T : (b + 1) * T]
    greet(
        [(lax.rem(d + p, D), r) for p in range(1, D)]
        + [(d, lax.rem(r + j, R)) for j in range(1, R)]
    )

    def halo(p):
        return rcopy(
            hsend.at[p], hrecv.at[p], h_s.at[p], h_r.at[p], lax.rem(d + p, D), r
        )

    def pick(p, dst):
        for k in range(K):
            dst[p, k] = blocks_of[slist[lax.rem(d + p, D), k]]

    def send_halo(p, carry):
        pick(p, hsend)
        halo(p).start()
        return carry

    lax.fori_loop(1, D, send_halo, 0)
    pick(0, hrecv)
    weight_copies = []
    for j in range(1, R):
        to = lax.rem(r + j, R)
        weight_copies.append(
            rcopy(wts_in, wts.at[r], ws_s.at[j], ws_r.at[j], d, to)
        )
        weight_copies.append(
            rcopy(wtn_in, wtn.at[r], wn_s.at[j], wn_r.at[j], d, to)
        )
    for copy in weight_copies:
        copy.start()
    feat_copy = rcopy(feats, xf.at[c], xf_s, xf_r, d, mate)
    feat_copy.start()
    wts[r] = wts_in[...]
    wtn[r] = wtn_in[...]
    xf[c] = feats[...]

    ones = jnp.ones((ONES, T), BF16)
    ones_wide = jnp.ones((ONES, L * T), BF16)
    loads[0].wait()

    def near(b, carry):
        left = jnp.concatenate(
            [
                blocks_of[cols[b, l]]
                for l in range(L)
            ],
            axis=1,
        )
        left = jnp.concatenate([left, ones_wide], axis=0)
        right = jnp.concatenate([ltiles[b, l] for l in range(L)], axis=1)
        summed[b] = mm_nt(left, right)[: F + KEEP]
        return carry

    lax.fori_loop(0, B, near, 0, unroll=4)
    loads[1].wait()

    def far_step(p, carry):
        source = lax.rem(d - p + D, D)
        for k in range(K):
            left = jnp.concatenate([hrecv[p, k], ones], axis=0)
            far[p * K + k] = mm_nt(left, rtiles[source, k])[: F + KEEP]
        return carry

    def far_wait(p, carry):
        halo(p).wait_recv()
        return carry

    far_step(0, 0)
    lax.fori_loop(1, D, far_wait, 0)
    lax.fori_loop(1, D, far_step, 0, unroll=7)

    agg_copies = []
    for ch in range(CHUNKS):

        def place(i, carry):
            b = ch * CB + i
            total = summed[b]

            def add(p, total):
                source = lax.rem(d - p + D, D)
                for k in range(K):
                    hit = place_at[source * K + k, b]
                    total = total + far[p * K + k] * hit
                return total

            total = lax.fori_loop(0, D, add, total, unroll=8)
            inverse = 1.0 / (1.0 + total[F:])
            at = pl.multiple_of(i * T, T)
            whole_at = pl.multiple_of(b * T, T)
            inv[:, pl.ds(whole_at, T)] = inverse
            xa[ch, c, :, pl.ds(at, T)] = (total[:F] * inverse[:1]).astype(BF16)
            return carry

        lax.fori_loop(0, CB, place, 0)
        copy = rcopy(xa.at[ch, c], xa.at[ch, c], xa_s.at[ch], xa_r.at[ch], d, mate)
        copy.start()
        agg_copies.append(copy)

    for copy in weight_copies:
        copy.wait_recv()
    chip = pl.ds(pl.multiple_of(g * 2 * F, 2 * F), 2 * F)
    for i, ref in enumerate((wts, wtn)):
        block = ref[:, :, chip].reshape(R * F, 2 * F)
        turned = block.astype(F32).T.astype(BF16)
        wb[i] = turned.reshape(2, F, R * F)
    lefts = []
    for q in range(G):
        t = cross(q)
        lefts.append(jnp.concatenate([wts[t, :, chip], wtn[t, :, chip]], axis=1))
    left = jnp.concatenate(lefts, axis=0)
    feat_copy.wait_recv()

    def stacked(ch):
        near_part = xf[:, :, ch * CH : (ch + 1) * CH].reshape(2 * F, CH)
        return jnp.concatenate([near_part, xa[ch].reshape(2 * F, CH)], axis=0)

    part_copies = []
    for ch in range(CHUNKS):
        agg_copies[ch].wait_recv()
        part = mm(left, stacked(ch))
        for q in range(1, G):
            psend[q, ch] = part[q * F : (q + 1) * F].astype(BF16)
            copy = rcopy(
                psend.at[q, ch],
                precv.at[q, ch],
                pp_s.at[q, ch],
                pp_r.at[q, ch],
                d,
                cross(q),
            )
            copy.start()
            part_copies.append(copy)
        own[ch] = part[:F]

    loads[2].wait()
    cross_copies, mate_copies = [], []
    for ch in range(CHUNKS):
        preact = own[ch]
        for q in range(1, G):
            part_copies[ch * (G - 1) + q - 1].wait_recv()
            preact = preact + precv[q, ch].astype(F32)
        s = jax.nn.sigmoid(preact)
        at = slice(ch * CH, (ch + 1) * CH)
        out_o[:, at] = (preact * s).astype(BF16)
        slope = s * (1.0 + preact * (1.0 - s))
        gp[ch, r] = (cot[:, at].astype(F32) * slope).astype(BF16)
        for q in range(1, G):
            copy = rcopy(
                gp.at[ch, r],
                gp.at[ch, r],
                gx_s.at[q, ch],
                gx_r.at[q, ch],
                d,
                cross(q),
            )
            copy.start()
            cross_copies.append(copy)
        copy = rcopy(
            gp.at[ch, r], gp.at[ch, r], gc_s.at[0, ch], gc_r.at[0, ch], d, mate
        )
        copy.start()
        mate_copies.append(copy)

    grads = jnp.zeros((G * F, 4 * F), F32)
    for ch in range(CHUNKS):
        blocks = [gp[ch, r]]
        for q in range(1, G):
            cross_copies[ch * (G - 1) + q - 1].wait_recv()
            t = lax.rem(g - q + G, G) * 2 + c
            copy = rcopy(
                gp.at[ch, t], gp.at[ch, t], gc_s.at[q, ch], gc_r.at[q, ch], d, mate
            )
            copy.start()
            mate_copies.append(copy)
        for q in range(1, G):
            blocks.append(gp[ch, cross(q)])
        grads = grads + mm_nt(jnp.concatenate(blocks, axis=0), stacked(ch))
    rows = gw_o.shape[2]
    for p in range(D):
        for q in range(G):
            gw_o[p, q] = grads[q * F + p * rows : q * F + (p + 1) * rows]

    for copy in mate_copies:
        copy.wait_recv()
    back_left = jnp.concatenate([wb[0, c], wb[1, c]], axis=0)
    for ch in range(CHUNKS):
        at = slice(ch * CH, (ch + 1) * CH)
        back = mm(back_left, gp[ch].reshape(R * F, CH))
        bself_o[:, at] = back[:F]
        scaled_o[:, at] = (back[F:] * inv[:1, at]).astype(BF16)

    def drain(p, carry):
        halo(p).wait_send()
        return carry

    lax.fori_loop(1, D, drain, 0)
    for copy in (
        weight_copies
        + [feat_copy]
        + agg_copies
        + part_copies
        + cross_copies
        + mate_copies
    ):
        copy.wait_send()


def scatter_kernel(cols, rrows, scaled, bself, ltiles, rtiles, acc_o, ret_o):
    F, N = scaled.shape
    B, L, T, _ = ltiles.shape
    D, K = rrows.shape
    acc_o[...] = bself[...]

    def near(b, carry):
        left = scaled[:, pl.ds(pl.multiple_of(b * T, T), T)]
        right = jnp.concatenate([ltiles[b, l] for l in range(L)], axis=1)
        back = mm(left, right)
        for l in range(L):
            at = pl.ds(pl.multiple_of(cols[b, l] * T, T), T)
            acc_o[:, at] = acc_o[:, at] + back[:, l * T : (l + 1) * T]
        return carry

    lax.fori_loop(0, B, near, 0, unroll=4)

    def away(s, carry):
        for k in range(K):
            left = scaled[:, pl.ds(pl.multiple_of(rrows[s, k] * T, T), T)]
            ret_o[s, k] = mm(left, rtiles[s, k]).astype(BF16)
        return carry

    lax.fori_loop(0, D, away, 0, unroll=4)


def return_kernel(
    D,
    R,
    home_at,
    acc,
    ret,
    gw,
    gf_o,
    gs_o,
    gn_o,
    back,
    gpart,
    red,
    final,
    h_s,
    h_r,
    p_s,
    p_r,
    f_s,
    f_r,
):
    d, r = lax.axis_index("dom"), lax.axis_index("rep")
    G = R // 2
    c, g = lax.rem(r, 2), lax.div(r, 2)
    F, N = acc.shape
    _, K, _, T = ret.shape
    B = N // T
    rows = gw.shape[2]

    def cross(q):
        return lax.rem(g + q, G) * 2 + c

    greet(
        [
            (lax.rem(d + p, D), cross(q))
            for q in range(G)
            for p in range(D)
            if p or q
        ]
    )
    pieces, halos, finals = [], [], []
    for p in range(1, D):
        to = lax.rem(d + p, D)
        copy = rcopy(gw.at[to], gpart.at[p], p_s.at[p], p_r.at[p], to, r)
        copy.start()
        pieces.append(copy)
    for p in range(1, D):
        to = lax.rem(d + p, D)
        copy = rcopy(ret.at[to], back.at[p], h_s.at[p], h_r.at[p], to, r)
        copy.start()
        halos.append(copy)
    total = gw[d]
    back[0] = ret[d]
    for p in range(1, D):
        pieces[p - 1].wait_recv()
        total = total + gpart[p]
    red[...] = total
    for q in range(G):
        for p in range(D):
            if p or q:
                copy = rcopy(
                    red.at[q],
                    final.at[g, d],
                    f_s.at[q, p],
                    f_r.at[q, p],
                    lax.rem(d + p, D),
                    cross(q),
                )
                copy.start()
                finals.append(copy)
    final[g, d] = red[0]
    for copy in halos:
        copy.wait_recv()

    def home(b, carry):
        at = pl.ds(pl.multiple_of(b * T, T), T)

        def add(p, total):
            source = lax.rem(d - p + D, D)
            for k in range(K):
                hit = home_at[source * K + k, b]
                total = total + back[p, k].astype(F32) * hit
            return total

        total = lax.fori_loop(0, D, add, acc[:, at], unroll=8)
        gf_o[:, at] = total.astype(BF16)
        return carry

    lax.fori_loop(0, B, home, 0)
    for copy in finals:
        copy.wait_recv()
    for h in range(G):
        at = slice(h * 2 * F, (h + 1) * 2 * F)
        for p in range(D):
            piece = final[h, p]
            where = slice(p * rows, (p + 1) * rows)
            gs_o[where, at] = piece[:, : 2 * F]
            gn_o[where, at] = piece[:, 2 * F :]
    for copy in pieces + halos + finals:
        copy.wait_send()


def local(
    D,
    R,
    feats,
    w_self,
    w_neigh,
    local_cols,
    local_tiles,
    send_list,
    remote_rows,
    remote_tiles,
    cotangent,
):
    F, N = feats.shape
    B, L, T, _ = local_tiles.shape
    K = send_list.shape[2]
    G = R // 2
    CH = N // CHUNKS
    rows = F // D
    vmem = pl.BlockSpec(memory_space=pltpu.VMEM)
    smem = pl.BlockSpec(memory_space=pltpu.SMEM)
    hbm = pl.BlockSpec(memory_space=pl.ANY)
    dma = pltpu.SemaphoreType.DMA
    slist, rrows = send_list[0], remote_rows[0]
    far_tiles = remote_tiles[0]
    ids = jnp.arange(B, dtype=jnp.int32)
    place_at = (rrows.reshape(D * K, 1) == ids).astype(F32)
    home_at = (slist.reshape(D * K, 1) == ids).astype(F32)
    limit = 60 * 1024 * 1024
    output, scaled, bself, gw = pl.pallas_call(
        functools.partial(main_kernel, D, R),
        out_shape=(
            jax.ShapeDtypeStruct((F, N), BF16),
            jax.ShapeDtypeStruct((F, N), BF16),
            jax.ShapeDtypeStruct((F, N), F32),
            jax.ShapeDtypeStruct((D, G, rows, 4 * F), F32),
        ),
        in_specs=[vmem, vmem, vmem, smem, smem, smem, hbm, hbm, hbm],
        out_specs=(vmem, vmem, vmem, vmem),
        scratch_shapes=[
            pltpu.VMEM((B, L, T, T), BF16),
            pltpu.VMEM((D, K, T, T), BF16),
            pltpu.VMEM((F, N), BF16),
            pltpu.VMEM((B, F, T), BF16),
            pltpu.VMEM((D, K, F, T), BF16),
            pltpu.VMEM((D, K, F, T), BF16),
            pltpu.VMEM((B, F + KEEP, T), F32),
            pltpu.VMEM((D * K, F + KEEP, T), F32),
            pltpu.VMEM((KEEP, N), F32),
            pltpu.VMEM((R, F, R * F), BF16),
            pltpu.VMEM((R, F, R * F), BF16),
            pltpu.VMEM((2, 2, F, R * F), BF16),
            pltpu.VMEM((2, F, N), BF16),
            pltpu.VMEM((CHUNKS, 2, F, CH), BF16),
            pltpu.VMEM((CHUNKS, F, CH), F32),
            pltpu.VMEM((G, CHUNKS, F, CH), BF16),
            pltpu.VMEM((G, CHUNKS, F, CH), BF16),
            pltpu.VMEM((CHUNKS, R, F, CH), BF16),
            dma((3,)),
            dma((D,)),
            dma((D,)),
            dma((R,)),
            dma((R,)),
            dma((R,)),
            dma((R,)),
            dma,
            dma,
            dma((CHUNKS,)),
            dma((CHUNKS,)),
            dma((G, CHUNKS)),
            dma((G, CHUNKS)),
            dma((G, CHUNKS)),
            dma((G, CHUNKS)),
            dma((G, CHUNKS)),
            dma((G, CHUNKS)),
        ],
        compiler_params=pltpu.CompilerParams(
            collective_id=0, has_side_effects=True, vmem_limit_bytes=limit
        ),
        name="layer_main",
    )(
        feats,
        w_self.T,
        w_neigh.T,
        local_cols,
        slist,
        place_at,
        local_tiles,
        far_tiles,
        cotangent,
    )
    acc, ret = pl.pallas_call(
        scatter_kernel,
        out_shape=(
            jax.ShapeDtypeStruct((F, N), F32),
            jax.ShapeDtypeStruct((D, K, F, T), BF16),
        ),
        in_specs=[smem, smem, vmem, vmem, vmem, vmem],
        out_specs=(vmem, vmem),
        compiler_params=pltpu.CompilerParams(vmem_limit_bytes=limit),
        name="tile_scatter",
    )(local_cols, rrows, scaled, bself, local_tiles, far_tiles)
    grad_feats, gs, gn = pl.pallas_call(
        functools.partial(return_kernel, D, R),
        out_shape=(
            jax.ShapeDtypeStruct((F, N), BF16),
            jax.ShapeDtypeStruct((F, R * F), F32),
            jax.ShapeDtypeStruct((F, R * F), F32),
        ),
        in_specs=[smem, vmem, vmem, vmem],
        out_specs=(vmem, vmem, vmem),
        scratch_shapes=[
            pltpu.VMEM((D, K, F, T), BF16),
            pltpu.VMEM((D, G, rows, 4 * F), F32),
            pltpu.VMEM((G, rows, 4 * F), F32),
            pltpu.VMEM((G, D, rows, 4 * F), F32),
            dma((D,)),
            dma((D,)),
            dma((D,)),
            dma((D,)),
            dma((G, D)),
            dma((G, D)),
        ],
        compiler_params=pltpu.CompilerParams(
            collective_id=1, has_side_effects=True, vmem_limit_bytes=limit
        ),
        name="return_sums",
    )(home_at, acc, ret, gw)
    return output, grad_feats, gs.T, gn.T


def solution(mesh):
    placed = (
        P("rep", "dom"),
        P(None, "rep"),
        P(None, "rep"),
        P("dom", None),
        P("dom", None, None, None),
        P("dom", None, None),
        P("dom", None, None),
        P("dom", None, None, None, None),
        P("rep", "dom"),
    )
    return jax.shard_map(
        functools.partial(local, mesh.shape["dom"], mesh.shape["rep"]),
        mesh=mesh,
        in_specs=placed,
        out_specs=(P("rep", "dom"), P("rep", "dom"), P(None, "rep"), P(None, "rep")),
        check_vma=False,
    )
```

time: 200 us -> 80.6 us (0.40)
  waiting for transfers between devices: 125 us -> 0 us
  Pallas kernels: 0 us -> 70 us
  matrix products: 23.3 us -> 0 us
  between operations: 14 us -> 0.7 us
  starting transfers between devices: 13 us -> 0 us
  blocking collectives: 11 us -> 0 us
  local copies, waits for them, and re-layouts: 10.5 us -> 8.33 us
    pallas_call x0 -> x3, Pallas kernels: none -> 70 us  [the longest x1 43.3 us: local(): pl.pallas_call(functools.partial(main_kernel, D, R), out_shape=(jax.Shape...]
    psum x1 -> x0, waiting for transfers between devices: 56.8 us -> none  [local(): wg_self, wg_neigh = lax.psum((wg_self, wg_neigh), 'dom')]
    all_gather x3 -> x0, waiting for transfers between devices: 53.1 us -> none  [the longest x1 21.1 us: local(): full_feats = lax.all_gather(feats, 'rep', axis=0, tiled=True)]
    dot_general x14 -> x0, matrix products: 23.3 us -> none  [the longest x1 3.59 us: local(): jnp.einsum('ab,an->bn', w_self, full_feats, preferred_element_type=jnp.fl...]
    all_to_all x2 -> x0, waiting for transfers between devices: 13.9 us -> none  [the longest x1 8.12 us: local(): lax.all_to_all(far_back, 'dom', split_axis=1, concat_axis=1, tiled=True)]
    all_to_all x2 -> x0, starting transfers between devices: 12.8 us -> none  [the longest x1 7.31 us: local(): lax.all_to_all(outgoing, 'dom', split_axis=1, concat_axis=1, tiled=True)]
    all_gather x2 -> x0, blocking collectives: 11 us -> none  [the longest x1 5.6 us: local(): lax.all_gather(w_neigh, 'rep', axis=1, tiled=True)]
    gather x3 -> x0, local copies, waits for them, and re-layouts: 4.71 us -> none  [the longest x1 1.76 us: local(): picked = scaled[:, far_rows]]
  transfers between devices with their start and end apart: 6 -> 0, of which waited for: 6 -> 0; matrix products, arithmetic and copies ran while one was open for 9% -> 0% of each run, Pallas kernels for 0% -> 0%
where the time goes in v1:
time: 80.6 us; the launch traced here: 80.4 us
  Pallas kernels  70 us (87%)
  local copies, waits for them, and re-layouts  8.33 us (10%)
  other arithmetic  1.35 us (2%)
    pallas_call x1, Pallas kernels, local(): pl.pallas_call(functools.partial(main_kernel, D, R), out_shape=(jax.Shape...  43.3 us
    pallas_call x1, Pallas kernels, local(): pl.pallas_call(functools.partial(return_kernel, D, R), out_shape=(jax.Sha...  21.4 us
    unnamed x17, local copies, waits for them, and re-layouts  6.15 us
    pallas_call x1, Pallas kernels, local(): pl.pallas_call(scatter_kernel, out_shape=(jax.ShapeDtypeStruct((F, N), F3...  5.25 us
    squeeze x2, local copies, waits for them, and re-layouts, local(): slist, rrows = (send_list[0], remote_rows[0])  2.02 us

profile of v1, /device:TPU:0, one launch (start us, length us, event | category | flops | bytes accessed | tf_op | source)
XLA Modules:
  0.0 80.4 jit_solution(9556879582614415004)
XLA Ops:
  0.6 0.0 copy-start.3
  0.6 1.4 %copy.20.cols = s32[32,2]{1,0:T(8,128)} copy(s32[32,2]{0,1:T(2,128)} %param.12) | data formatting | bytes 512 | tf_op args[3]
  2.0 0.8 copy.19
  2.8 0.1 eq.30
  2.8 0.7 fusion.place_at
  3.5 1.3 %copy.21.slist = s32[8,2]{1,0:T(8,128)} copy(s32[8,2]{0,1:T(2,128)} %bitcast.14) | data formatting | bytes 128 | tf_op jit(solution)/shard_map/squeeze | solution.py:481
  4.9 43.3 %layer_main.1 = (bf16[64,4096]{1,0:T(8,128)(2,1)}, bf16[64,4096]{1,0:T(8,128)(2,1)}, f32[64,4096]{1,0:T(8,128)}, f32[8,2,8,256]{3,2,1,0:T(8,128)}) custom-call(bf16[64,4096]{1,0:T(8,128)(2,1)} %feats.1, bf16[64,256]{1,0:T(8,128)(2,1)} %bitcast.11, bf16[64,256]{1,0:T(8,128)(2,1)} %bitcast.12, s32[32,2]{1,0:T(8,128)} %copy.20.cols, s32[8,2]{1,0:T(8,128)} %copy.21.slist, ...), custom_call_target="tpu_custom_call" | custom-call | tf_op jit(solution)/shard_map/layer_main/pallas_call | solution.py:487
  48.2 0.0 copy-done.3
  48.2 0.7 copy.24.rrows
  48.9 0.0 copy-start.4
  48.9 0.0 copy-start
  48.9 5.3 %tile_scatter.1 = (f32[64,4096]{1,0:T(8,128)}, bf16[8,2,64,128]{3,2,1,0:T(8,128)(2,1)}) custom-call(s32[32,2]{1,0:T(8,128)} %copy.20.cols, s32[8,2]{1,0:T(8,128)} %copy.24.rrows, bf16[64,4096]{1,0:T(8,128)(2,1)} %get-tuple-element.14.scaled, f32[64,4096]{1,0:T(8,128)} %get-tuple-element.15.bself, bf16[32,2,128,128]{3,2,1,0:T(8,128)(2,1)} %ltiles.1, ...), custom_call_target="tpu_custom_call" | custom-call | tf_op jit(solution)/shard_map/tile_scatter/pallas_call | solution.py:549
  54.2 0.0 copy-done.4
  54.2 0.1 copy.22
  54.3 0.1 eq.34
  54.3 0.7 fusion.1.home_at
  55.0 21.4 %return_sums.1 = (bf16[64,4096]{1,0:T(8,128)(2,1)}, f32[64,256]{1,0:T(8,128)}, f32[64,256]{1,0:T(8,128)}) custom-call(f32[16,32]{1,0:T(8,128)} %fusion.1.home_at, f32[64,4096]{1,0:T(8,128)} %get-tuple-element.16.acc, bf16[8,2,64,128]{3,2,1,0:T(8,128)(2,1)} %get-tuple-element.17.ret, f32[8,2,8,256]{3,2,1,0:T(8,128)} %get-tuple-element.18.gw), custom_call_target="tpu_custom_call" | custom-call | tf_op jit(solution)/shard_map/return_sums/pallas_call | solution.py:560
  76.4 0.0 copy-start.2
  76.4 0.0 copy-start.1
  76.4 0.0 copy-done
  76.4 0.8 copy.29
  77.2 1.9 %copy.30 = bf16[64,4096]{1,0:T(8,128)(2,1)} copy(bf16[64,4096]{1,0:T(8,128)(2,1)} %get-tuple-element.27) | data formatting | bytes 1048576
  79.1 0.0 copy-done.2
  79.1 0.6 copy.31
  79.7 0.0 copy-done.1
  79.7 0.6 copy.32
Async XLA Ops:
  0.6 47.6 %copy-start.3 = (s32[1,8,2]{1,2,0:T(2,128)S(1)}, s32[1,8,2]{1,2,0:T(2,128)}, u32[]{:S(2)}) copy-start(s32[1,8,2]{1,2,0:T(2,128)} %param.15) | copy-start | bytes 196
  48.9 5.3 %copy-start.4 = (s32[1,8,2]{1,2,0:T(2,128)S(1)}, s32[1,8,2]{1,2,0:T(2,128)}, u32[]{:S(2)}) copy-start(s32[1,8,2]{1,2,0:T(2,128)} %param.14) | copy-start | bytes 196
  48.9 27.5 %copy-start = (bf16[64,4096]{1,0:T(8,128)(2,1)S(1)}, bf16[64,4096]{1,0:T(8,128)(2,1)}, u32[]{:S(2)}) copy-start(bf16[64,4096]{1,0:T(8,128)(2,1)} %get-tuple-element.26) | copy-start | bytes 1572868
  76.4 2.7 %copy-start.2 = (f32[64,256]{1,0:T(8,128)S(1)}, f32[64,256]{1,0:T(8,128)}, u32[]{:S(2)}) copy-start(f32[64,256]{1,0:T(8,128)} %get-tuple-element.20) | copy-start | bytes 196612
  76.4 3.3 %copy-start.1 = (f32[64,256]{1,0:T(8,128)S(1)}, f32[64,256]{1,0:T(8,128)}, u32[]{:S(2)}) copy-start(f32[64,256]{1,0:T(8,128)} %get-tuple-element.21) | copy-start | bytes 196612

commit v2 on v1

--- a/solution.py
+++ b/solution.py
@@ -22,6 +22,11 @@
 
 def mm_nt(a, b):
     return lax.dot_general(a, b, NT, preferred_element_type=F32)
+
+
+def equal_one(x, y):
+    gap = x - y
+    return (1 - jnp.minimum(gap * gap, 1)).astype(F32)
 
 
 def rcopy(src, dst, send, recv, dom, rep):
@@ -52,14 +57,14 @@
     wtn_in,
     cols,
     slist,
-    place_at,
+    rrows,
     ltiles_h,
     rtiles_h,
     cot_h,
     out_o,
-    scaled_o,
-    bself_o,
-    gw_o,
+    acc_o,
+    back_o,
+    final_o,
     ltiles,
     rtiles,
     cot,
@@ -78,6 +83,12 @@
     psend,
     precv,
     gp,
+    gw,
+    gpart,
+    red,
+    scaled,
+    ret,
+    nearb,
     loc_sem,
     h_s,
     h_r,
@@ -95,6 +106,12 @@
     gx_r,
     gc_s,
     gc_r,
+    b_s,
+    b_r,
+    p_s,
+    p_r,
+    f_s,
+    f_r,
 ):
     d, r = lax.axis_index("dom"), lax.axis_index("rep")
     G = R // 2
@@ -102,7 +119,7 @@
     mate = g * 2 + 1 - c
     F, N = feats.shape
     B, L, T, _ = ltiles.shape
-    K = slist.shape[1]
+    K = slist.shape[0]
     CH = N // CHUNKS
     CB = B // CHUNKS
 
@@ -119,8 +136,13 @@
     for b in range(B):
         blocks_of[b] = feats[:, b * T : (b + 1) * T]
     greet(
-        [(lax.rem(d + p, D), r) for p in range(1, D)]
-        + [(d, lax.rem(r + j, R)) for j in range(1, R)]
+        [
+            (lax.rem(d + p, D), cross(q))
+            for q in range(G)
+            for p in range(D)
+            if p or q
+        ]
+        + [(d, lax.rem(g + q, G) * 2 + 1 - c) for q in range(G)]
     )
 
     def halo(p):
@@ -130,7 +152,7 @@
 
     def pick(p, dst):
         for k in range(K):
-            dst[p, k] = blocks_of[slist[lax.rem(d + p, D), k]]
+            dst[p, k] = blocks_of[slist[k, lax.rem(d + p, D)]]
 
     def send_halo(p, carry):
         pick(p, hsend)
@@ -163,7 +185,7 @@
     def near(b, carry):
         left = jnp.concatenate(
             [
-                blocks_of[cols[b, l]]
+                blocks_of[cols[l, b]]
                 for l in range(L)
             ],
             axis=1,
@@ -201,7 +223,7 @@
             def add(p, total):
                 source = lax.rem(d - p + D, D)
                 for k in range(K):
-                    hit = place_at[source * K + k, b]
+                    hit = equal_one(rrows[k, source], b)
                     total = total + far[p * K + k] * hit
                 return total
 
@@ -297,19 +319,103 @@
         for q in range(1, G):
             blocks.append(gp[ch, cross(q)])
         grads = grads + mm_nt(jnp.concatenate(blocks, axis=0), stacked(ch))
-    rows = gw_o.shape[2]
+    rows = gw.shape[2]
     for p in range(D):
         for q in range(G):
-            gw_o[p, q] = grads[q * F + p * rows : q * F + (p + 1) * rows]
-
-    for copy in mate_copies:
-        copy.wait_recv()
+            gw[p, q] = grads[q * F + p * rows : q * F + (p + 1) * rows]
+
+    def piece(p):
+        to = lax.rem(d + p, D)
+        return rcopy(gw.at[to], gpart.at[p], p_s.at[p], p_r.at[p], to, r)
+
+    def send_piece(p, carry):
+        piece(p).start()
+        return carry
+
+    lax.fori_loop(1, D, send_piece, 0)
+
     back_left = jnp.concatenate([wb[0, c], wb[1, c]], axis=0)
     for ch in range(CHUNKS):
-        at = slice(ch * CH, (ch + 1) * CH)
+        later = CHUNKS + ch * (G - 1)
+        for copy in [mate_copies[ch]] + mate_copies[later : later + G - 1]:
+            copy.wait_recv()
         back = mm(back_left, gp[ch].reshape(R * F, CH))
-        bself_o[:, at] = back[:F]
-        scaled_o[:, at] = (back[F:] * inv[:1, at]).astype(BF16)
+        for i in range(CB):
+            b = ch * CB + i
+            at = slice(i * T, (i + 1) * T)
+            whole_at = slice(b * T, (b + 1) * T)
+            acc_o[:, whole_at] = back[:F, at]
+            scaled[b] = (back[F:, at] * inv[:1, whole_at]).astype(BF16)
+
+    def away(p, dst, slot):
+        source = lax.rem(d + p, D)
+        for k in range(K):
+            block = scaled[rrows[k, source]]
+            dst[slot, k] = mm(block, rtiles[source, k]).astype(BF16)
+
+    def returned(p):
+        to = lax.rem(d + p, D)
+        return rcopy(ret.at[p], back_o.at[d], b_s.at[p], b_r.at[p], to, r)
+
+    def send_back(p, carry):
+        away(p, ret, p)
+        returned(p).start()
+        return carry
+
+    lax.fori_loop(1, D, send_back, 0, unroll=7)
+    away(0, back_o, d)
+
+    def take_piece(p, total):
+        piece(p).wait_recv()
+        return total + gpart[p]
+
+    red[...] = lax.fori_loop(1, D, take_piece, gw[d])
+    finals = []
+    for q in range(G):
+        for p in range(D):
+            if p or q:
+                copy = rcopy(
+                    red.at[q],
+                    final_o.at[g, d],
+                    f_s.at[q, p],
+                    f_r.at[q, p],
+                    lax.rem(d + p, D),
+                    cross(q),
+                )
+                copy.start()
+                finals.append(copy)
+    final_o[g, d] = red[0]
+
+    def near_back(b, carry):
+        right = jnp.concatenate([ltiles[b, l] for l in range(L)], axis=1)
+        both = mm(scaled[b], right)
+        for l in range(L):
+            nearb[l, b] = both[:, l * T : (l + 1) * T]
+        return carry
+
+    lax.fori_loop(0, B, near_back, 0, unroll=4)
+
+    def gather_back(block, carry):
+        at = pl.ds(pl.multiple_of(block * T, T), T)
+
+        def add(b, total):
+            for l in range(L):
+                total = total + nearb[l, b] * equal_one(cols[l, b], block)
+            return total
+
+        acc_o[:, at] = lax.fori_loop(0, B, add, acc_o[:, at], unroll=8)
+        return carry
+
+    lax.fori_loop(0, B, gather_back, 0)
+
+    def finish_back(p, carry):
+        returned(p).wait()
+        piece(p).wait_send()
+        return carry
+
+    lax.fori_loop(1, D, finish_back, 0)
+    for copy in finals:
+        copy.wait_recv()
 
     def drain(p, carry):
         halo(p).wait_send()
@@ -323,136 +429,34 @@
         + part_copies
         + cross_copies
         + mate_copies
+        + finals
     ):
         copy.wait_send()
 
 
-def scatter_kernel(cols, rrows, scaled, bself, ltiles, rtiles, acc_o, ret_o):
-    F, N = scaled.shape
-    B, L, T, _ = ltiles.shape
-    D, K = rrows.shape
-    acc_o[...] = bself[...]
-
-    def near(b, carry):
-        left = scaled[:, pl.ds(pl.multiple_of(b * T, T), T)]
-        right = jnp.concatenate([ltiles[b, l] for l in range(L)], axis=1)
-        back = mm(left, right)
-        for l in range(L):
-            at = pl.ds(pl.multiple_of(cols[b, l] * T, T), T)
-            acc_o[:, at] = acc_o[:, at] + back[:, l * T : (l + 1) * T]
-        return carry
-
-    lax.fori_loop(0, B, near, 0, unroll=4)
-
-    def away(s, carry):
+def finish_kernel(slist, acc, back, final, out, out_o, gf_o, gs_o, gn_o, total):
+    F, N = acc.shape
+    D, K, _, T = back.shape
+    G, _, rows, width = final.shape
+    half = width // 2
+    out_o[...] = out[...]
+    total[...] = acc[...]
+
+    def home(s, carry):
         for k in range(K):
-            left = scaled[:, pl.ds(pl.multiple_of(rrows[s, k] * T, T), T)]
-            ret_o[s, k] = mm(left, rtiles[s, k]).astype(BF16)
-        return carry
-
-    lax.fori_loop(0, D, away, 0, unroll=4)
-
-
-def return_kernel(
-    D,
-    R,
-    home_at,
-    acc,
-    ret,
-    gw,
-    gf_o,
-    gs_o,
-    gn_o,
-    back,
-    gpart,
-    red,
-    final,
-    h_s,
-    h_r,
-    p_s,
-    p_r,
-    f_s,
-    f_r,
-):
-    d, r = lax.axis_index("dom"), lax.axis_index("rep")
-    G = R // 2
-    c, g = lax.rem(r, 2), lax.div(r, 2)
-    F, N = acc.shape
-    _, K, _, T = ret.shape
-    B = N // T
-    rows = gw.shape[2]
-
-    def cross(q):
-        return lax.rem(g + q, G) * 2 + c
-
-    greet(
-        [
-            (lax.rem(d + p, D), cross(q))
-            for q in range(G)
-            for p in range(D)
-            if p or q
-        ]
-    )
-    pieces, halos, finals = [], [], []
-    for p in range(1, D):
-        to = lax.rem(d + p, D)
-        copy = rcopy(gw.at[to], gpart.at[p], p_s.at[p], p_r.at[p], to, r)
-        copy.start()
-        pieces.append(copy)
-    for p in range(1, D):
-        to = lax.rem(d + p, D)
-        copy = rcopy(ret.at[to], back.at[p], h_s.at[p], h_r.at[p], to, r)
-        copy.start()
-        halos.append(copy)
-    total = gw[d]
-    back[0] = ret[d]
-    for p in range(1, D):
-        pieces[p - 1].wait_recv()
-        total = total + gpart[p]
-    red[...] = total
-    for q in range(G):
+            at = pl.ds(pl.multiple_of(slist[k, s] * T, T), T)
+            total[:, at] = total[:, at] + back[s, k].astype(F32)
+        return carry
+
+    lax.fori_loop(0, D, home, 0)
+    gf_o[...] = total[...].astype(BF16)
+    for h in range(G):
+        at = slice(h * half, (h + 1) * half)
         for p in range(D):
-            if p or q:
-                copy = rcopy(
-                    red.at[q],
-                    final.at[g, d],
-                    f_s.at[q, p],
-                    f_r.at[q, p],
-                    lax.rem(d + p, D),
-                    cross(q),
-                )
-                copy.start()
-                finals.append(copy)
-    final[g, d] = red[0]
-    for copy in halos:
-        copy.wait_recv()
-
-    def home(b, carry):
-        at = pl.ds(pl.multiple_of(b * T, T), T)
-
-        def add(p, total):
-            source = lax.rem(d - p + D, D)
-            for k in range(K):
-                hit = home_at[source * K + k, b]
-                total = total + back[p, k].astype(F32) * hit
-            return total
-
-        total = lax.fori_loop(0, D, add, acc[:, at], unroll=8)
-        gf_o[:, at] = total.astype(BF16)
-        return carry
-
-    lax.fori_loop(0, B, home, 0)
-    for copy in finals:
-        copy.wait_recv()
-    for h in range(G):
-        at = slice(h * 2 * F, (h + 1) * 2 * F)
-        for p in range(D):
-            piece = final[h, p]
+            part = final[h, p]
             where = slice(p * rows, (p + 1) * rows)
-            gs_o[where, at] = piece[:, : 2 * F]
-            gn_o[where, at] = piece[:, 2 * F :]
-    for copy in pieces + halos + finals:
-        copy.wait_send()
+            gs_o[where, at] = part[:, :half]
+            gn_o[where, at] = part[:, half:]
 
 
 def local(
@@ -478,19 +482,17 @@
     smem = pl.BlockSpec(memory_space=pltpu.SMEM)
     hbm = pl.BlockSpec(memory_space=pl.ANY)
     dma = pltpu.SemaphoreType.DMA
-    slist, rrows = send_list[0], remote_rows[0]
+    slist = jnp.swapaxes(send_list, 1, 2)[0]
+    rrows = jnp.swapaxes(remote_rows, 1, 2)[0]
     far_tiles = remote_tiles[0]
-    ids = jnp.arange(B, dtype=jnp.int32)
-    place_at = (rrows.reshape(D * K, 1) == ids).astype(F32)
-    home_at = (slist.reshape(D * K, 1) == ids).astype(F32)
     limit = 60 * 1024 * 1024
-    output, scaled, bself, gw = pl.pallas_call(
+    output, acc, back, final = pl.pallas_call(
         functools.partial(main_kernel, D, R),
         out_shape=(
             jax.ShapeDtypeStruct((F, N), BF16),
-            jax.ShapeDtypeStruct((F, N), BF16),
             jax.ShapeDtypeStruct((F, N), F32),
-            jax.ShapeDtypeStruct((D, G, rows, 4 * F), F32),
+            jax.ShapeDtypeStruct((D, K, F, T), BF16),
+            jax.ShapeDtypeStruct((G, D, rows, 4 * F), F32),
         ),
         in_specs=[vmem, vmem, vmem, smem, smem, smem, hbm, hbm, hbm],
         out_specs=(vmem, vmem, vmem, vmem),
@@ -513,6 +515,12 @@
             pltpu.VMEM((G, CHUNKS, F, CH), BF16),
             pltpu.VMEM((G, CHUNKS, F, CH), BF16),
             pltpu.VMEM((CHUNKS, R, F, CH), BF16),
+            pltpu.VMEM((D, G, rows, 4 * F), F32),
+            pltpu.VMEM((D, G, rows, 4 * F), F32),
+            pltpu.VMEM((G, rows, 4 * F), F32),
+            pltpu.VMEM((B, F, T), BF16),
+            pltpu.VMEM((D, K, F, T), BF16),
+            pltpu.VMEM((L, B, F, T), F32),
             dma((3,)),
             dma((D,)),
             dma((D,)),
@@ -530,6 +538,12 @@
             dma((G, CHUNKS)),
             dma((G, CHUNKS)),
             dma((G, CHUNKS)),
+            dma((D,)),
+            dma((D,)),
+            dma((D,)),
+            dma((D,)),
+            dma((G, D)),
+            dma((G, D)),
         ],
         compiler_params=pltpu.CompilerParams(
             collective_id=0, has_side_effects=True, vmem_limit_bytes=limit
@@ -539,50 +553,27 @@
         feats,
         w_self.T,
         w_neigh.T,
-        local_cols,
+        local_cols.T,
         slist,
-        place_at,
+        rrows,
         local_tiles,
         far_tiles,
         cotangent,
     )
-    acc, ret = pl.pallas_call(
-        scatter_kernel,
+    output, grad_feats, gs, gn = pl.pallas_call(
+        finish_kernel,
         out_shape=(
-            jax.ShapeDtypeStruct((F, N), F32),
-            jax.ShapeDtypeStruct((D, K, F, T), BF16),
-        ),
-        in_specs=[smem, smem, vmem, vmem, vmem, vmem],
-        out_specs=(vmem, vmem),
-        compiler_params=pltpu.CompilerParams(vmem_limit_bytes=limit),
-        name="tile_scatter",
-    )(local_cols, rrows, scaled, bself, local_tiles, far_tiles)
-    grad_feats, gs, gn = pl.pallas_call(
-        functools.partial(return_kernel, D, R),
-        out_shape=(
+            jax.ShapeDtypeStruct((F, N), BF16),
             jax.ShapeDtypeStruct((F, N), BF16),
             jax.ShapeDtypeStruct((F, R * F), F32),
             jax.ShapeDtypeStruct((F, R * F), F32),
         ),
-        in_specs=[smem, vmem, vmem, vmem],
-        out_specs=(vmem, vmem, vmem),
-        scratch_shapes=[
-            pltpu.VMEM((D, K, F, T), BF16),
-            pltpu.VMEM((D, G, rows, 4 * F), F32),
-            pltpu.VMEM((G, rows, 4 * F), F32),
-            pltpu.VMEM((G, D, rows, 4 * F), F32),
-            dma((D,)),
-            dma((D,)),
-            dma((D,)),
-            dma((D,)),
-            dma((G, D)),
-            dma((G, D)),
-        ],
-        compiler_params=pltpu.CompilerParams(
-            collective_id=1, has_side_effects=True, vmem_limit_bytes=limit
-        ),
-        name="return_sums",
-    )(home_at, acc, ret, gw)
+        in_specs=[smem, vmem, vmem, vmem, vmem],
+        out_specs=(vmem, vmem, vmem, vmem),
+        scratch_shapes=[pltpu.VMEM((F, N), F32)],
+        compiler_params=pltpu.CompilerParams(vmem_limit_bytes=limit // 4),
+        name="finish",
+    )(slist, acc, back, final, output)
     return output, grad_feats, gs.T, gn.T
 
 

time: 80.6 us -> 65.2 us (0.81)
  Pallas kernels: 70 us -> 60.1 us
  local copies, waits for them, and re-layouts: 8.33 us -> 4.12 us
  other arithmetic: 1.35 us -> 0 us
    pallas_call x2 -> x1, Pallas kernels: 26.6 us -> 1.79 us  [local(): pl.pallas_call(finish_kernel, out_shape=(jax.ShapeDtypeStruct((F, N), BF1...]
    pallas_call x1, Pallas kernels: 43.3 us -> 58.3 us  [local(): pl.pallas_call(functools.partial(main_kernel, D, R), out_shape=(jax.Shape...]
    unnamed x17 -> x10, local copies, waits for them, and re-layouts: 6.15 us -> 4.12 us
    squeeze x2 -> x0, local copies, waits for them, and re-layouts: 2.02 us -> none  [local(): slist, rrows = (send_list[0], remote_rows[0])]
    convert_element_type x2 -> x0, other arithmetic: 1.35 us -> none  [the longest x1 0.68 us: local(): home_at = (slist.reshape(D * K, 1) == ids).astype(F32)]
where the time goes in v2:
time: 65.2 us; the launch traced here: 64.9 us
  Pallas kernels  60.1 us (92%)
  local copies, waits for them, and re-layouts  4.12 us (6%)
  between operations  0.67 us (1%)
    pallas_call x1, Pallas kernels, local(): pl.pallas_call(functools.partial(main_kernel, D, R), out_shape=(jax.Shape...  58.3 us
    unnamed x10, local copies, waits for them, and re-layouts  4.12 us
    pallas_call x1, Pallas kernels, local(): pl.pallas_call(finish_kernel, out_shape=(jax.ShapeDtypeStruct((F, N), BF1...  1.79 us

profile of v2, /device:TPU:0, one launch (start us, length us, event | category | flops | bytes accessed | tf_op | source)
XLA Modules:
  0.0 64.9 jit_solution(1263750711982432978)
XLA Ops:
  0.6 0.0 copy-start.4
  0.6 58.3 %layer_main.1 = (bf16[64,4096]{1,0:T(8,128)(2,1)}, f32[64,4096]{1,0:T(8,128)}, bf16[8,2,64,128]{3,2,1,0:T(8,128)(2,1)}, f32[2,8,8,256]{3,2,1,0:T(8,128)}) custom-call(bf16[64,4096]{1,0:T(8,128)(2,1)} %feats.1, bf16[64,256]{1,0:T(8,128)(2,1)} %bitcast.15, bf16[64,256]{1,0:T(8,128)(2,1)} %bitcast.16, s32[2,32]{1,0:T(2,128)} %bitcast.17, s32[2,8]{1,0:T(2,128)} %bitcast.12, ...), custom_call_target="tpu_custom_call" | custom-call | tf_op jit(solution)/shard_map/layer_main/pallas_call | solution.py:489
  59.0 0.0 copy-done.4
  59.0 0.0 copy-start
  59.0 1.2 %copy-done = f32[64,4096]{1,0:T(8,128)S(1)} copy-done((f32[64,4096]{1,0:T(8,128)S(1)}, f32[64,4096]{1,0:T(8,128)}, u32[]{:S(2)}) %copy-start) | copy-done | bytes 1048600
  60.2 0.0 copy-start.1
  60.2 1.0 %copy-done.1 = bf16[64,4096]{1,0:T(8,128)(2,1)S(1)} copy-done((bf16[64,4096]{1,0:T(8,128)(2,1)S(1)}, bf16[64,4096]{1,0:T(8,128)(2,1)}, u32[]{:S(2)}) %copy-start.1) | copy-done | bytes 524312
  61.2 0.0 copy-start.2
  61.2 0.9 %copy-done.2 = bf16[8,2,64,128]{3,2,1,0:T(8,128)(2,1)S(1)} copy-done((bf16[8,2,64,128]{3,2,1,0:T(8,128)(2,1)S(1)}, bf16[8,2,64,128]{3,2,1,0:T(8,128)(2,1)}, u32[]{:S(2)}) %copy-start.2) | copy-done | bytes 262168
  62.2 0.0 copy-start.3
  62.2 0.9 %copy-done.3 = f32[2,8,8,256]{3,2,1,0:T(8,128)S(1)} copy-done((f32[2,8,8,256]{3,2,1,0:T(8,128)S(1)}, f32[2,8,8,256]{3,2,1,0:T(8,128)}, u32[]{:S(2)}) %copy-start.3) | copy-done | bytes 131096
  63.1 1.8 %finish.1 = (bf16[64,4096]{1,0:T(8,128)(2,1)}, bf16[64,4096]{1,0:T(8,128)(2,1)}, f32[64,256]{1,0:T(8,128)}, f32[64,256]{1,0:T(8,128)}) custom-call(s32[2,8]{1,0:T(2,128)S(1)} %bitcast.13, f32[64,4096]{1,0:T(8,128)S(1)} %copy-done, bf16[8,2,64,128]{3,2,1,0:T(8,128)(2,1)S(1)} %copy-done.2, f32[2,8,8,256]{3,2,1,0:T(8,128)S(1)} %copy-done.3, ...), custom_call_target="tpu_custom_call" | custom-call | tf_op jit(solution)/shard_map/finish/pallas_call | solution.py:563
Async XLA Ops:
  0.6 58.3 %copy-start.4 = (s32[1,8,2]{1,2,0:T(2,128)S(1)}, s32[1,8,2]{1,2,0:T(2,128)}, u32[]{:S(2)}) copy-start(s32[1,8,2]{1,2,0:T(2,128)} %param.14) | copy-start | bytes 196
  59.0 1.2 %copy-start = (f32[64,4096]{1,0:T(8,128)S(1)}, f32[64,4096]{1,0:T(8,128)}, u32[]{:S(2)}) copy-start(f32[64,4096]{1,0:T(8,128)} %get-tuple-element.12.acc) | copy-start | bytes 3145732
  60.2 1.0 %copy-start.1 = (bf16[64,4096]{1,0:T(8,128)(2,1)S(1)}, bf16[64,4096]{1,0:T(8,128)(2,1)}, u32[]{:S(2)}) copy-start(bf16[64,4096]{1,0:T(8,128)(2,1)} %get-tuple-element.15.out) | copy-start | bytes 1572868
  61.2 0.9 %copy-start.2 = (bf16[8,2,64,128]{3,2,1,0:T(8,128)(2,1)S(1)}, bf16[8,2,64,128]{3,2,1,0:T(8,128)(2,1)}, u32[]{:S(2)}) copy-start(bf16[8,2,64,128]{3,2,1,0:T(8,128)(2,1)} %get-tuple-element.13.back) | copy-start | bytes 786436
  62.2 0.9 %copy-start.3 = (f32[2,8,8,256]{3,2,1,0:T(8,128)S(1)}, f32[2,8,8,256]{3,2,1,0:T(8,128)}, u32[]{:S(2)}) copy-start(f32[2,8,8,256]{3,2,1,0:T(8,128)} %get-tuple-element.14.final) | copy-start | bytes 393220

commit v3 on v2

--- a/solution.py
+++ b/solution.py
@@ -161,21 +161,27 @@
 
     lax.fori_loop(1, D, send_halo, 0)
     pick(0, hrecv)
-    weight_copies = []
-    for j in range(1, R):
-        to = lax.rem(r + j, R)
+    weight_copies, cross_weights = [], []
+    sets = ((wts_in, wts, ws_s, ws_r), (wtn_in, wtn, wn_s, wn_r))
+    chip = pl.ds(pl.multiple_of(g * 2 * F, 2 * F), 2 * F)
+    for q in range(1, G):
+        there = lax.rem(g + q, G)
+        cut = pl.ds(pl.multiple_of(there * 2 * F, 2 * F), 2 * F)
+        for src, dst, ss, rs in sets:
+            cross_weights.append(
+                rcopy(src.at[:, cut], dst.at[r], ss.at[q], rs.at[q], d, cross(q))
+            )
+    for src, dst, ss, rs in sets:
         weight_copies.append(
-            rcopy(wts_in, wts.at[r], ws_s.at[j], ws_r.at[j], d, to)
+            rcopy(src.at[:, chip], dst.at[r], ss.at[0], rs.at[0], d, mate)
         )
-        weight_copies.append(
-            rcopy(wtn_in, wtn.at[r], wn_s.at[j], wn_r.at[j], d, to)
-        )
-    for copy in weight_copies:
+    for copy in cross_weights + weight_copies:
         copy.start()
     feat_copy = rcopy(feats, xf.at[c], xf_s, xf_r, d, mate)
     feat_copy.start()
-    wts[r] = wts_in[...]
-    wtn[r] = wtn_in[...]
+    wts[r] = wts_in[:, chip]
+    wtn[r] = wtn_in[:, chip]
+    acc_o[...] = jnp.zeros((F, N), F32)
     xf[c] = feats[...]
 
     ones = jnp.ones((ONES, T), BF16)
@@ -196,6 +202,15 @@
         return carry
 
     lax.fori_loop(0, B, near, 0, unroll=4)
+    for copy in cross_weights:
+        copy.wait_recv()
+    for q in range(1, G):
+        t = lax.rem(g - q + G, G) * 2 + c
+        for _, dst, ss, rs in sets:
+            slot = G + q - 1
+            copy = rcopy(dst.at[t], dst.at[t], ss.at[slot], rs.at[slot], d, mate)
+            copy.start()
+            weight_copies.append(copy)
     loads[1].wait()
 
     def far_step(p, carry):
@@ -242,15 +257,14 @@
 
     for copy in weight_copies:
         copy.wait_recv()
-    chip = pl.ds(pl.multiple_of(g * 2 * F, 2 * F), 2 * F)
     for i, ref in enumerate((wts, wtn)):
-        block = ref[:, :, chip].reshape(R * F, 2 * F)
+        block = ref[...].reshape(R * F, 2 * F)
         turned = block.astype(F32).T.astype(BF16)
         wb[i] = turned.reshape(2, F, R * F)
     lefts = []
     for q in range(G):
         t = cross(q)
-        lefts.append(jnp.concatenate([wts[t, :, chip], wtn[t, :, chip]], axis=1))
+        lefts.append(jnp.concatenate([wts[t], wtn[t]], axis=1))
     left = jnp.concatenate(lefts, axis=0)
     feat_copy.wait_recv()
 
@@ -305,6 +319,46 @@
         copy.start()
         mate_copies.append(copy)
 
+    back_left = jnp.concatenate([wb[0, c], wb[1, c]], axis=0)
+
+    def back_chunk(ch):
+        later = CHUNKS + ch * (G - 1)
+        for copy in [mate_copies[ch]] + mate_copies[later : later + G - 1]:
+            copy.wait_recv()
+        back = mm(back_left, gp[ch].reshape(R * F, CH))
+        for i in range(CB):
+            b = ch * CB + i
+            at = slice(i * T, (i + 1) * T)
+            whole_at = slice(b * T, (b + 1) * T)
+            acc_o[:, whole_at] += back[:F, at]
+            scaled[b] = (back[F:, at] * inv[:1, whole_at]).astype(BF16)
+
+    def scatter_chunk(ch):
+        first = ch * CB
+
+        def near_back(i, carry):
+            b = first + i
+            right = jnp.concatenate([ltiles[b, l] for l in range(L)], axis=1)
+            both = mm(scaled[b], right)
+            for l in range(L):
+                nearb[l, i] = both[:, l * T : (l + 1) * T]
+            return carry
+
+        lax.fori_loop(0, CB, near_back, 0, unroll=4)
+
+        def gather_back(block, carry):
+            at = pl.ds(pl.multiple_of(block * T, T), T)
+
+            def add(i, total):
+                for l in range(L):
+                    total = total + nearb[l, i] * equal_one(cols[l, first + i], block)
+                return total
+
+            acc_o[:, at] = lax.fori_loop(0, CB, add, acc_o[:, at], unroll=8)
+            return carry
+
+        lax.fori_loop(0, B, gather_back, 0)
+
     grads = jnp.zeros((G * F, 4 * F), F32)
     for ch in range(CHUNKS):
         blocks = [gp[ch, r]]
@@ -319,6 +373,10 @@
         for q in range(1, G):
             blocks.append(gp[ch, cross(q)])
         grads = grads + mm_nt(jnp.concatenate(blocks, axis=0), stacked(ch))
+        if ch >= 1:
+            back_chunk(ch - 1)
+        if ch >= 1 and ch + 1 < CHUNKS:
+            scatter_chunk(ch - 1)
     rows = gw.shape[2]
     for p in range(D):
         for q in range(G):
@@ -334,18 +392,7 @@
 
     lax.fori_loop(1, D, send_piece, 0)
 
-    back_left = jnp.concatenate([wb[0, c], wb[1, c]], axis=0)
-    for ch in range(CHUNKS):
-        later = CHUNKS + ch * (G - 1)
-        for copy in [mate_copies[ch]] + mate_copies[later : later + G - 1]:
-            copy.wait_recv()
-        back = mm(back_left, gp[ch].reshape(R * F, CH))
-        for i in range(CB):
-            b = ch * CB + i
-            at = slice(i * T, (i + 1) * T)
-            whole_at = slice(b * T, (b + 1) * T)
-            acc_o[:, whole_at] = back[:F, at]
-            scaled[b] = (back[F:, at] * inv[:1, whole_at]).astype(BF16)
+    back_chunk(CHUNKS - 1)
 
     def away(p, dst, slot):
         source = lax.rem(d + p, D)
@@ -386,27 +433,8 @@
                 finals.append(copy)
     final_o[g, d] = red[0]
 
-    def near_back(b, carry):
-        right = jnp.concatenate([ltiles[b, l] for l in range(L)], axis=1)
-        both = mm(scaled[b], right)
-        for l in range(L):
-            nearb[l, b] = both[:, l * T : (l + 1) * T]
-        return carry
-
-    lax.fori_loop(0, B, near_back, 0, unroll=4)
-
-    def gather_back(block, carry):
-        at = pl.ds(pl.multiple_of(block * T, T), T)
-
-        def add(b, total):
-            for l in range(L):
-                total = total + nearb[l, b] * equal_one(cols[l, b], block)
-            return total
-
-        acc_o[:, at] = lax.fori_loop(0, B, add, acc_o[:, at], unroll=8)
-        return carry
-
-    lax.fori_loop(0, B, gather_back, 0)
+    for ch in range(max(CHUNKS - 2, 0), CHUNKS):
+        scatter_chunk(ch)
 
     def finish_back(p, carry):
         returned(p).wait()
@@ -424,6 +452,7 @@
     lax.fori_loop(1, D, drain, 0)
     for copy in (
         weight_copies
+        + cross_weights
         + [feat_copy]
         + agg_copies
         + part_copies
@@ -434,13 +463,23 @@
         copy.wait_send()
 
 
-def finish_kernel(slist, acc, back, final, out, out_o, gf_o, gs_o, gn_o, total):
-    F, N = acc.shape
+def finish_kernel(
+    slist, acc_h, back_h, final_h, out_h, out_o, gf_o, gs_o, gn_o, total, back, final, sem
+):
+    F, N = acc_h.shape
+    loads = [
+        pltpu.make_async_copy(src, dst, sem.at[i])
+        for i, (src, dst) in enumerate(
+            ((out_h, out_o), (acc_h, total), (back_h, back), (final_h, final))
+        )
+    ]
+    for load in loads:
+        load.start()
     D, K, _, T = back.shape
     G, _, rows, width = final.shape
     half = width // 2
-    out_o[...] = out[...]
-    total[...] = acc[...]
+    for load in loads[1:]:
+        load.wait()
 
     def home(s, carry):
         for k in range(K):
@@ -457,6 +496,7 @@
             where = slice(p * rows, (p + 1) * rows)
             gs_o[where, at] = part[:, :half]
             gn_o[where, at] = part[:, half:]
+    loads[0].wait()
 
 
 def local(
@@ -506,8 +546,8 @@
             pltpu.VMEM((B, F + KEEP, T), F32),
             pltpu.VMEM((D * K, F + KEEP, T), F32),
             pltpu.VMEM((KEEP, N), F32),
-            pltpu.VMEM((R, F, R * F), BF16),
-            pltpu.VMEM((R, F, R * F), BF16),
+            pltpu.VMEM((R, F, 2 * F), BF16),
+            pltpu.VMEM((R, F, 2 * F), BF16),
             pltpu.VMEM((2, 2, F, R * F), BF16),
             pltpu.VMEM((2, F, N), BF16),
             pltpu.VMEM((CHUNKS, 2, F, CH), BF16),
@@ -520,7 +560,7 @@
             pltpu.VMEM((G, rows, 4 * F), F32),
             pltpu.VMEM((B, F, T), BF16),
             pltpu.VMEM((D, K, F, T), BF16),
-            pltpu.VMEM((L, B, F, T), F32),
+            pltpu.VMEM((L, B // CHUNKS, F, T), F32),
             dma((3,)),
             dma((D,)),
             dma((D,)),
@@ -568,10 +608,15 @@
             jax.ShapeDtypeStruct((F, R * F), F32),
             jax.ShapeDtypeStruct((F, R * F), F32),
         ),
-        in_specs=[smem, vmem, vmem, vmem, vmem],
+        in_specs=[smem, hbm, hbm, hbm, hbm],
         out_specs=(vmem, vmem, vmem, vmem),
-        scratch_shapes=[pltpu.VMEM((F, N), F32)],
-        compiler_params=pltpu.CompilerParams(vmem_limit_bytes=limit // 4),
+        scratch_shapes=[
+            pltpu.VMEM((F, N), F32),
+            pltpu.VMEM((D, K, F, T), BF16),
+            pltpu.VMEM((G, D, rows, 4 * F), F32),
+            dma((4,)),
+        ],
+        compiler_params=pltpu.CompilerParams(vmem_limit_bytes=limit),
         name="finish",
     )(slist, acc, back, final, output)
     return output, grad_feats, gs.T, gn.T

time: 65.2 us -> 63.4 us (0.972)
  local copies, waits for them, and re-layouts: 4.12 us -> 0 us
  Pallas kernels: 60.1 us -> 62.6 us
    unnamed x10 -> x0, local copies, waits for them, and re-layouts: 4.12 us -> none
    pallas_call x1, Pallas kernels: 1.79 us -> 3.37 us  [local(): pl.pallas_call(finish_kernel, out_shape=(jax.ShapeDtypeStruct((F, N), BF1...]
    pallas_call x1, Pallas kernels: 58.3 us -> 59.2 us  [local(): pl.pallas_call(functools.partial(main_kernel, D, R), out_shape=(jax.Shape...]
where the time goes in v3:
time: 63.4 us; the launch traced here: 63.2 us
  Pallas kernels  62.6 us (99%)
  between operations  0.64 us (1%)
    pallas_call x1, Pallas kernels, local(): pl.pallas_call(functools.partial(main_kernel, D, R), out_shape=(jax.Shape...  59.2 us
    pallas_call x1, Pallas kernels, local(): pl.pallas_call(finish_kernel, out_shape=(jax.ShapeDtypeStruct((F, N), BF1...  3.37 us

profile of v3, /device:TPU:0, one launch (start us, length us, event | category | flops | bytes accessed | tf_op | source)
XLA Modules:
  0.0 63.2 jit_solution(3994342051353188814)
XLA Ops:
  0.6 59.2 %layer_main.1 = (bf16[64,4096]{1,0:T(8,128)(2,1)}, f32[64,4096]{1,0:T(8,128)}, bf16[8,2,64,128]{3,2,1,0:T(8,128)(2,1)}, f32[2,8,8,256]{3,2,1,0:T(8,128)}) custom-call(bf16[64,4096]{1,0:T(8,128)(2,1)} %feats.1, bf16[64,256]{1,0:T(8,128)(2,1)} %bitcast.13, bf16[64,256]{1,0:T(8,128)(2,1)} %bitcast.14, s32[2,32]{1,0:T(2,128)} %bitcast.17, s32[2,8]{1,0:T(2,128)} %bitcast.15, ...), custom_call_target="tpu_custom_call" | custom-call | tf_op jit(solution)/shard_map/layer_main/pallas_call | solution.py:529
  59.8 3.4 %finish.1 = (bf16[64,4096]{1,0:T(8,128)(2,1)}, bf16[64,4096]{1,0:T(8,128)(2,1)}, f32[64,256]{1,0:T(8,128)}, f32[64,256]{1,0:T(8,128)}) custom-call(s32[2,8]{1,0:T(2,128)} %bitcast.16, f32[64,4096]{1,0:T(8,128)} %get-tuple-element.12.acc_h, bf16[8,2,64,128]{3,2,1,0:T(8,128)(2,1)} %get-tuple-element.13.back_h, f32[2,8,8,256]{3,2,1,0:T(8,128)} %get-tuple-element.14.final_h, ...), custom_call_target="tpu_custom_call" | custom-call | tf_op jit(solution)/shard_map/finish/pallas_call | solution.py:603

commit v4 on v3

--- a/solution.py
+++ b/solution.py
@@ -181,7 +181,6 @@
     feat_copy.start()
     wts[r] = wts_in[:, chip]
     wtn[r] = wtn_in[:, chip]
-    acc_o[...] = jnp.zeros((F, N), F32)
     xf[c] = feats[...]
 
     ones = jnp.ones((ONES, T), BF16)
@@ -330,31 +329,28 @@
             b = ch * CB + i
             at = slice(i * T, (i + 1) * T)
             whole_at = slice(b * T, (b + 1) * T)
-            acc_o[:, whole_at] += back[:F, at]
+            acc_o[:, whole_at] = back[:F, at]
             scaled[b] = (back[F:, at] * inv[:1, whole_at]).astype(BF16)
 
-    def scatter_chunk(ch):
-        first = ch * CB
-
-        def near_back(i, carry):
-            b = first + i
+    def scatter_all():
+        def near_back(b, carry):
             right = jnp.concatenate([ltiles[b, l] for l in range(L)], axis=1)
             both = mm(scaled[b], right)
             for l in range(L):
-                nearb[l, i] = both[:, l * T : (l + 1) * T]
+                nearb[l, b] = both[:, l * T : (l + 1) * T]
             return carry
 
-        lax.fori_loop(0, CB, near_back, 0, unroll=4)
+        lax.fori_loop(0, B, near_back, 0, unroll=4)
 
         def gather_back(block, carry):
             at = pl.ds(pl.multiple_of(block * T, T), T)
 
             def add(i, total):
                 for l in range(L):
-                    total = total + nearb[l, i] * equal_one(cols[l, first + i], block)
+                    total = total + nearb[l, i] * equal_one(cols[l, i], block)
                 return total
 
-            acc_o[:, at] = lax.fori_loop(0, CB, add, acc_o[:, at], unroll=8)
+            acc_o[:, at] = lax.fori_loop(0, B, add, acc_o[:, at], unroll=8)
             return carry
 
         lax.fori_loop(0, B, gather_back, 0)
@@ -375,8 +371,6 @@
         grads = grads + mm_nt(jnp.concatenate(blocks, axis=0), stacked(ch))
         if ch >= 1:
             back_chunk(ch - 1)
-        if ch >= 1 and ch + 1 < CHUNKS:
-            scatter_chunk(ch - 1)
     rows = gw.shape[2]
     for p in range(D):
         for q in range(G):
@@ -433,8 +427,7 @@
                 finals.append(copy)
     final_o[g, d] = red[0]
 
-    for ch in range(max(CHUNKS - 2, 0), CHUNKS):
-        scatter_chunk(ch)
+    scatter_all()
 
     def finish_back(p, carry):
         returned(p).wait()
@@ -560,7 +553,7 @@
             pltpu.VMEM((G, rows, 4 * F), F32),
             pltpu.VMEM((B, F, T), BF16),
             pltpu.VMEM((D, K, F, T), BF16),
-            pltpu.VMEM((L, B // CHUNKS, F, T), F32),
+            pltpu.VMEM((L, B, F, T), F32),
             dma((3,)),
             dma((D,)),
             dma((D,)),

time: 63.4 us -> 62.6 us (0.987)
  Pallas kernels: 62.6 us -> 61.7 us
    pallas_call x1, Pallas kernels: 59.2 us -> 58.4 us  [local(): pl.pallas_call(functools.partial(main_kernel, D, R), out_shape=(jax.Shape...]
where the time goes in v4:
time: 62.6 us; the launch traced here: 62.4 us
  Pallas kernels  61.7 us (99%)
  between operations  0.64 us (1%)
    pallas_call x1, Pallas kernels, local(): pl.pallas_call(functools.partial(main_kernel, D, R), out_shape=(jax.Shape...  58.4 us
    pallas_call x1, Pallas kernels, local(): pl.pallas_call(finish_kernel, out_shape=(jax.ShapeDtypeStruct((F, N), BF1...  3.37 us

profile of v4, /device:TPU:0, one launch (start us, length us, event | category | flops | bytes accessed | tf_op | source)
XLA Modules:
  0.0 62.4 jit_solution(1152844338692277384)
XLA Ops:
  0.6 58.4 %layer_main.1 = (bf16[64,4096]{1,0:T(8,128)(2,1)}, f32[64,4096]{1,0:T(8,128)}, bf16[8,2,64,128]{3,2,1,0:T(8,128)(2,1)}, f32[2,8,8,256]{3,2,1,0:T(8,128)}) custom-call(bf16[64,4096]{1,0:T(8,128)(2,1)} %feats.1, bf16[64,256]{1,0:T(8,128)(2,1)} %bitcast.13, bf16[64,256]{1,0:T(8,128)(2,1)} %bitcast.14, s32[2,32]{1,0:T(2,128)} %bitcast.17, s32[2,8]{1,0:T(2,128)} %bitcast.15, ...), custom_call_target="tpu_custom_call" | custom-call | tf_op jit(solution)/shard_map/layer_main/pallas_call | solution.py:522
  59.0 3.4 %finish.1 = (bf16[64,4096]{1,0:T(8,128)(2,1)}, bf16[64,4096]{1,0:T(8,128)(2,1)}, f32[64,256]{1,0:T(8,128)}, f32[64,256]{1,0:T(8,128)}) custom-call(s32[2,8]{1,0:T(2,128)} %bitcast.16, f32[64,4096]{1,0:T(8,128)} %get-tuple-element.12.acc_h, bf16[8,2,64,128]{3,2,1,0:T(8,128)(2,1)} %get-tuple-element.13.back_h, f32[2,8,8,256]{3,2,1,0:T(8,128)} %get-tuple-element.14.final_h, ...), custom_call_target="tpu_custom_call" | custom-call | tf_op jit(solution)/shard_map/finish/pallas_call | solution.py:596
